TPU v7x, 32 devices: a whole 2x2x4 slice. The times are simulated.
32 devices in a mesh: dp: 8 (over z, y), mp: 4 (over x, core).
Axes of the slice: x: 2, y: 2, z: 4, core: 2. Of those that a mesh axis runs over, the one named last changes fastest.
Arguments:
- token_ids: int32 [16384], P('dp'), may hold values from 0 to 8191
- seg_ids: int32 [16384], P('dp'), may hold values from 0 to 255, as said below
- timesteps: int32 [16384], P('dp'), may hold values from 0 to 1999
- noise: float32 [16384, 128], P('dp'), may hold values from -6 to 6
- table: bfloat16 [8192, 128], P('dp'), may hold values from -6 to 6
- w_in: bfloat16 [128, 768], replicated, may hold values from -0.5 to 0.5
- b_in: float32 [768], replicated, may hold values from -3 to 3
- w_time: bfloat16 [128, 768], replicated, may hold values from -0.5 to 0.5
- gain1: float32 [768], replicated, may hold values from 0.5 to 1.5
- shift1: float32 [768], replicated, may hold values from -2 to 2
- w_qkv: bfloat16 [3, 768, 768], P(None, None, 'mp'), may hold values from -0.21875 to 0.21875
- w_out: bfloat16 [768, 768], P('mp'), may hold values from -3.5 to 3.5
- gain2: float32 [768], replicated, may hold values from 0.5 to 1.5
- shift2: float32 [768], replicated, may hold values from -2 to 2
- w_up: bfloat16 [768, 3072], P(None, 'mp'), may hold values from -0.21875 to 0.21875
- b_up: float32 [3072], P('mp'), may hold values from -2 to 2
- w_down: bfloat16 [3072, 768], P('mp'), may hold values from -0.109375 to 0.109375
- b_down: float32 [768], replicated, may hold values from -2 to 2
- cotangent: float32 [16384, 768], P('dp'), may hold values from -6 to 6
Outputs:
- output: float32 [16384, 768], P('dp')
- grad_table: float32 [8192, 128], P('dp')
- grad_w_in: float32 [128, 768], replicated
- grad_b_in: float32 [768], replicated
- grad_w_time: float32 [128, 768], replicated
- grad_gain1: float32 [768], replicated
- grad_shift1: float32 [768], replicated
- grad_w_qkv: float32 [3, 768, 768], P(None, None, 'mp')
- grad_w_out: float32 [768, 768], P('mp')
- grad_gain2: float32 [768], replicated
- grad_shift2: float32 [768], replicated
- grad_w_up: float32 [768, 3072], P(None, 'mp')
- grad_b_up: float32 [3072], P('mp')
- grad_w_down: float32 [3072, 768], P('mp')
- grad_b_down: float32 [768], replicated
Inputs may be any that keep to these rules, and one draw needn't show every extreme that they name: `seg_ids`: slots fall into aligned runs of 1024; each run is either one document or 16 documents of 64 slots; ids never fall along the slots and differ between runs; the first run is one document and the last is split.
All inputs are finite; a program needn't handle non-finite values.
Results may differ from a plain program's by a relative error of at most 0.017.
Values may be sent and summed in bfloat16 or wider, within the bound.
No kernel may reach another device: no remote copies, remote signals or barrier semaphores. Data moves between devices by JAX's collectives and lax.ppermute only.
A program may use at most 192 MiB of HBM per device.

v0:
```python
import math
import jax
import jax.numpy as jnp
from jax import lax
from jax.sharding import PartitionSpec as P

HD = 64
TSTEPS = 2000
QBLK = 512
NEG_BIG = -1000000000.0


def layer_norm(inputs, gain_vec, shift_vec):
    row_mean = jnp.mean(inputs, axis=-1, keepdims=True)
    centred = inputs - row_mean
    variance = jnp.mean(centred * centred, axis=-1, keepdims=True)
    return centred * lax.rsqrt(variance + 1e-05) * gain_vec + shift_vec


def noise_rates(time_ids, horizon):
    fraction = time_ids.astype(jnp.float32) / horizon
    signal = 1.0 - jnp.sqrt(fraction + 0.0001)
    return (jnp.sqrt(signal), jnp.sqrt(1.0 - signal))


def time_features(time_ids, feat_width):
    half_width = feat_width // 2
    freq_table = jnp.exp(
        -math.log(10000.0) * jnp.arange(half_width, dtype=jnp.float32) / half_width
    )
    angles = time_ids.astype(jnp.float32)[:, None] * freq_table[None, :]
    return jnp.concatenate([jnp.sin(angles), jnp.cos(angles)], axis=1)


def gelu_exact(inputs):
    return jax.nn.gelu(inputs, approximate=False)


def block_rows(array_in, index, block_len):
    return lax.dynamic_slice_in_dim(array_in, index * block_len, block_len, 0)


def masked_scores(query_blk, key_blk, seg_query, seg_key):
    scaled = jnp.einsum(
        "qhd,khd->hqk", query_blk, key_blk, preferred_element_type=jnp.float32
    ) * query_blk.shape[-1] ** (-0.5)
    same_seg = seg_query[:, None] == seg_key[None, :]
    return jnp.where(same_seg[None], scaled, NEG_BIG)


def attend_forward(queries, keys_all, values_all, seg_ids, block_len):
    token_count, head_count, head_width = queries.shape
    block_count = token_count // block_len

    def query_block(q_index):
        query_blk = block_rows(queries, q_index, block_len)
        seg_query = block_rows(seg_ids, q_index, block_len)

        def stats_step(k_index, current):
            row_top, row_sum = current
            scores = masked_scores(
                query_blk,
                block_rows(keys_all, k_index, block_len),
                seg_query,
                block_rows(seg_ids, k_index, block_len),
            )
            new_top = jnp.maximum(row_top, jnp.max(scores, axis=-1))
            new_sum = row_sum * jnp.exp(row_top - new_top) + jnp.sum(
                jnp.exp(scores - new_top[:, :, None]), axis=-1
            )
            return (new_top, new_sum)

        start_stats = (
            jnp.full((head_count, block_len), NEG_BIG, jnp.float32),
            jnp.zeros((head_count, block_len), jnp.float32),
        )
        row_top, row_sum = lax.fori_loop(0, block_count, stats_step, start_stats)

        def value_step(k_index, current):
            scores = masked_scores(
                query_blk,
                block_rows(keys_all, k_index, block_len),
                seg_query,
                block_rows(seg_ids, k_index, block_len),
            )
            weights_bf = (jnp.exp(scores - row_top[:, :, None]) / row_sum[:, :, None]).astype(
                jnp.bfloat16
            )
            return current + jnp.einsum(
                "hqk,khd->qhd",
                weights_bf,
                block_rows(values_all, k_index, block_len),
                preferred_element_type=jnp.float32,
            )

        mixed_blk = lax.fori_loop(
            0, block_count, value_step, jnp.zeros((block_len, head_count, head_width), jnp.float32)
        )
        return (mixed_blk, row_top, row_sum)

    mixed_all, tops, sums = lax.map(query_block, jnp.arange(block_count))
    return (mixed_all.reshape(token_count, head_count, head_width), tops, sums)


def attend_backward(queries, keys_all, values_all, grad_mixed, seg_ids, tops, sums, block_len):
    token_count, head_count, head_width = queries.shape
    block_count = token_count // block_len
    scale_factor = head_width ** (-0.5)

    def query_step(q_index, totals):
        grad_q_all, grad_k_all, grad_v_all = totals
        query_blk = block_rows(queries, q_index, block_len)
        grad_blk = block_rows(grad_mixed, q_index, block_len)
        seg_query = block_rows(seg_ids, q_index, block_len)
        row_top = tops[q_index]
        row_sum = sums[q_index]

        def probs_for(k_index):
            key_blk = block_rows(keys_all, k_index, block_len)
            value_blk = block_rows(values_all, k_index, block_len)
            scores = masked_scores(
                query_blk, key_blk, seg_query, block_rows(seg_ids, k_index, block_len)
            )
            weights = jnp.exp(scores - row_top[:, :, None]) / row_sum[:, :, None]
            grad_weights = jnp.einsum(
                "qhd,khd->hqk", grad_blk, value_blk, preferred_element_type=jnp.float32
            )
            return (key_blk, weights, grad_weights)

        def delta_step(k_index, current):
            key_blk, weights, grad_weights = probs_for(k_index)
            return current + jnp.sum(grad_weights * weights, axis=-1)

        delta = lax.fori_loop(
            0, block_count, delta_step, jnp.zeros((head_count, block_len), jnp.float32)
        )

        def grad_step(k_index, current):
            grad_query, grad_keys, grad_values = current
            key_blk, weights, grad_weights = probs_for(k_index)
            grad_scores = (weights * (grad_weights - delta[:, :, None])).astype(jnp.bfloat16)
            grad_query = (
                grad_query
                + jnp.einsum(
                    "hqk,khd->qhd", grad_scores, key_blk, preferred_element_type=jnp.float32
                )
                * scale_factor
            )
            key_part = (
                jnp.einsum(
                    "hqk,qhd->khd", grad_scores, query_blk, preferred_element_type=jnp.float32
                )
                * scale_factor
            )
            value_part = jnp.einsum(
                "hqk,qhd->khd",
                weights.astype(jnp.bfloat16),
                grad_blk,
                preferred_element_type=jnp.float32,
            )
            grad_keys = lax.dynamic_update_slice_in_dim(
                grad_keys,
                block_rows(grad_keys, k_index, block_len) + key_part,
                k_index * block_len,
                0,
            )
            grad_values = lax.dynamic_update_slice_in_dim(
                grad_values,
                block_rows(grad_values, k_index, block_len) + value_part,
                k_index * block_len,
                0,
            )
            return (grad_query, grad_keys, grad_values)

        start_grads = (
            jnp.zeros((block_len, head_count, head_width), jnp.float32),
            grad_k_all,
            grad_v_all,
        )
        grad_query, grad_k_all, grad_v_all = lax.fori_loop(0, block_count, grad_step, start_grads)
        grad_q_all = lax.dynamic_update_slice_in_dim(grad_q_all, grad_query, q_index * block_len, 0)
        return (grad_q_all, grad_k_all, grad_v_all)

    zeros_all = jnp.zeros(queries.shape, jnp.float32)
    return lax.fori_loop(0, block_count, query_step, (zeros_all, zeros_all, zeros_all))


def body(
    token_ids,
    seg_ids,
    timesteps,
    noise,
    table,
    w_in,
    b_in,
    w_time,
    gain1,
    shift1,
    w_qkv,
    w_out,
    gain2,
    shift2,
    w_up,
    b_up,
    w_down,
    b_down,
    cotangent,
):
    whole_table = lax.all_gather(table, "dp", axis=0, tiled=True)
    table_full = whole_table.astype(jnp.float32)
    vocab_rows, embed_width = table_full.shape
    row_norms = jnp.sqrt(jnp.sum(table_full * table_full, axis=1) + 1e-06)
    mean_norm = jnp.mean(row_norms)
    factor = math.sqrt(embed_width) / mean_norm
    looked_up = jnp.take(table_full, token_ids, axis=0)
    clean_rows = looked_up * factor
    keep_rate, noise_rate = noise_rates(timesteps, TSTEPS)
    noisy_in = (keep_rate[:, None] * clean_rows + noise_rate[:, None] * noise).astype(jnp.bfloat16)
    features = time_features(timesteps, w_time.shape[0]).astype(jnp.bfloat16)
    hidden = (
        jnp.dot(noisy_in, w_in, preferred_element_type=jnp.float32)
        + jnp.dot(features, w_time, preferred_element_type=jnp.float32)
        + b_in
    )
    token_count = hidden.shape[0]
    act_one_f, norm_one_back = jax.vjp(layer_norm, hidden, gain1, shift1)
    act_one = act_one_f.astype(jnp.bfloat16)
    projected = jnp.einsum(
        "td,cdk->ctk", act_one, w_qkv, preferred_element_type=jnp.float32
    ).astype(jnp.bfloat16)
    head_count = w_qkv.shape[2] // HD
    heads_all = projected.reshape(3, token_count, head_count, HD)
    queries, keys_all, values_all = (heads_all[0], heads_all[1], heads_all[2])
    mixed_f, tops, sums = attend_forward(queries, keys_all, values_all, seg_ids, QBLK)
    mixed = mixed_f.astype(jnp.bfloat16).reshape(token_count, head_count * HD)
    attn_part = jnp.dot(mixed, w_out, preferred_element_type=jnp.float32)
    resid = hidden + lax.psum(attn_part, "mp")
    act_two_f, norm_two_back = jax.vjp(layer_norm, resid, gain2, shift2)
    act_two = act_two_f.astype(jnp.bfloat16)
    pre_act = jnp.dot(act_two, w_up, preferred_element_type=jnp.float32) + b_up
    activated_f, gelu_back = jax.vjp(gelu_exact, pre_act)
    activated = activated_f.astype(jnp.bfloat16)
    down_part = jnp.dot(activated, w_down, preferred_element_type=jnp.float32)
    output = resid + lax.psum(down_part.astype(jnp.bfloat16), "mp").astype(jnp.float32) + b_down
    cot_rounded = cotangent.astype(jnp.bfloat16)
    grad_w_down = jnp.einsum(
        "tf,td->fd", activated, cot_rounded, preferred_element_type=jnp.float32
    )
    grad_b_down = jnp.sum(cotangent, axis=0)
    grad_gelu = jnp.einsum("td,fd->tf", cot_rounded, w_down, preferred_element_type=jnp.float32)
    (grad_pre,) = gelu_back(grad_gelu)
    grad_pre_r = grad_pre.astype(jnp.bfloat16)
    grad_w_up = jnp.einsum("td,tf->df", act_two, grad_pre_r, preferred_element_type=jnp.float32)
    grad_b_up = jnp.sum(grad_pre_r.astype(jnp.float32), axis=0)
    grad_two_part = jnp.einsum("tf,df->td", grad_pre_r, w_up, preferred_element_type=jnp.float32)
    grad_act_two = lax.psum(grad_two_part, "mp")
    grad_resid_norm, grad_gain2, grad_shift2 = norm_two_back(grad_act_two)
    grad_resid = cotangent + grad_resid_norm
    grad_attn_r = grad_resid.astype(jnp.bfloat16)
    grad_w_out = jnp.einsum("tk,td->kd", mixed, grad_attn_r, preferred_element_type=jnp.float32)
    grad_mixed = (
        jnp.einsum("td,kd->tk", grad_attn_r, w_out, preferred_element_type=jnp.float32)
        .astype(jnp.bfloat16)
        .reshape(token_count, head_count, HD)
    )
    grad_q, grad_k, grad_v = attend_backward(
        queries, keys_all, values_all, grad_mixed, seg_ids, tops, sums, QBLK
    )
    grad_proj = jnp.stack(
        [grad_q.astype(jnp.bfloat16), grad_k.astype(jnp.bfloat16), grad_v.astype(jnp.bfloat16)]
    ).reshape(3, token_count, head_count * HD)
    grad_w_qkv = jnp.einsum("td,ctk->cdk", act_one, grad_proj, preferred_element_type=jnp.float32)
    grad_one_part = jnp.einsum("ctk,cdk->td", grad_proj, w_qkv, preferred_element_type=jnp.float32)
    grad_act_one = lax.psum(grad_one_part.astype(jnp.bfloat16), "mp").astype(jnp.float32)
    grad_hidden_norm, grad_gain1, grad_shift1 = norm_one_back(grad_act_one)
    grad_hidden_r = (grad_resid + grad_hidden_norm).astype(jnp.bfloat16)
    grad_w_in = jnp.einsum("te,td->ed", noisy_in, grad_hidden_r, preferred_element_type=jnp.float32)
    grad_w_time = jnp.einsum(
        "te,td->ed", features, grad_hidden_r, preferred_element_type=jnp.float32
    )
    grad_b_in = jnp.sum(grad_hidden_r.astype(jnp.float32), axis=0)
    grad_noisy = jnp.einsum("td,ed->te", grad_hidden_r, w_in, preferred_element_type=jnp.float32)
    grad_clean = keep_rate[:, None] * grad_noisy
    scaled_grad = grad_clean * factor
    norm_coeff = -jnp.sum(grad_clean * looked_up) * factor / (mean_norm * vocab_rows)
    unit_rows = table_full / row_norms[:, None]
    row_count = lax.axis_size("dp") * table.shape[0]
    inside = (token_ids >= 0) & (token_ids < row_count)
    slot_ids = jnp.where(inside, token_ids, row_count)
    direct = jax.ops.segment_sum(scaled_grad, slot_ids, num_segments=row_count + 1)[:row_count]
    grad_table = lax.psum_scatter(
        direct + norm_coeff * unit_rows, "dp", scatter_dimension=0, tiled=True
    )
    summed = tuple(
        lax.psum(
            (
                grad_w_in,
                grad_b_in,
                grad_w_time,
                grad_gain1,
                grad_shift1,
                grad_w_qkv,
                grad_w_out,
                grad_gain2,
                grad_shift2,
                grad_w_up,
                grad_b_up,
                grad_w_down,
                grad_b_down,
            ),
            "dp",
        )
    )
    return (
        output,
        grad_table,
        summed[0],
        summed[1],
        summed[2],
        summed[3],
        summed[4],
        summed[5],
        summed[6],
        summed[7],
        summed[8],
        summed[9],
        summed[10],
        summed[11],
        summed[12],
    )


def solution(mesh):
    in_specs = (
        P("dp"),
        P("dp"),
        P("dp"),
        P("dp", None),
        P("dp", None),
        P(),
        P(),
        P(),
        P(),
        P(),
        P(None, None, "mp"),
        P("mp", None),
        P(),
        P(),
        P(None, "mp"),
        P("mp"),
        P("mp", None),
        P(),
        P("dp", None),
    )
    out_specs = (
        P("dp", None),
        P("dp", None),
        P(),
        P(),
        P(),
        P(),
        P(),
        P(None, None, "mp"),
        P("mp", None),
        P(),
        P(),
        P(None, "mp"),
        P("mp"),
        P("mp", None),
        P(),
    )
    return jax.shard_map(body, mesh=mesh, in_specs=in_specs, out_specs=out_specs, check_vma=False)
```

profile of v0, /device:TPU:0, one launch (start us, length us, event | category | flops | bytes accessed | tf_op | source)
XLA Modules:
  0.0 1170.5 jit_solution(15731865098663500380)
XLA Ops:
  13.5 48.5 %all-gather.2.cloned.1.call-done = bf16[8192,128]{1,0:T(8,128)(2,1)} async-done(((bf16[1024,128]{1,0:T(8,128)(2,1)}), bf16[8192,128]{1,0:T(8,128)(2,1)}) %all-gather.2.cloned.1.call-update) | async-done | bytes 2097168 | tf_op jit(solution)/shard_map/all_gather | solution.py:209
  90.6 98.2 %while.123 = (s32[]{:T(128)}, bf16[4,512,3,64]{1,3,2,0:T(8,128)(2,1)}, f32[4,3,512]{2,1,0:T(4,128)}, f32[4,3,512]{2,1,0:T(4,128)}, s32[4]{0:T(128)S(1)}, /*index...) while((s32[]{:T(128)}, ...), condition=%wide.region_11.12_spmd, body=%wide.region_4.11_spmd.sunk | while | flops 312155648 | bytes 10699101 | solution.py:101
  100.9 12.5 %while.128 = (s32[]{:T(128)}, f32[512,3,64]{0,2,1:T(8,128)}, bf16[2048,3,64]{0,2,1:T(8,128)(2,1)S(1)}, s32[512]{0:T(512)S(1)}, s32[2048]{0:T(1024)S(1)}, /*index...) while((s32[]{:T(128)}, f32[512,3,64]{0,2,1:T(8,128)}, ...), condition=%wide.region_10.10_spmd.clone, body=%wide.region_9.9_spmd.clone.sunk | while | flops 205717504 | bytes 1926848 | solution.py:96
  125.4 12.5 %while.128 = (s32[]{:T(128)}, f32[512,3,64]{0,2,1:T(8,128)}, bf16[2048,3,64]{0,2,1:T(8,128)(2,1)S(1)}, s32[512]{0:T(512)S(1)}, s32[2048]{0:T(1024)S(1)}, /*index...) while((s32[]{:T(128)}, f32[512,3,64]{0,2,1:T(8,128)}, ...), condition=%wide.region_10.10_spmd.clone, body=%wide.region_9.9_spmd.clone.sunk | while | flops 205717504 | bytes 1926848 | solution.py:96
  149.8 12.5 %while.128 = (s32[]{:T(128)}, f32[512,3,64]{0,2,1:T(8,128)}, bf16[2048,3,64]{0,2,1:T(8,128)(2,1)S(1)}, s32[512]{0:T(512)S(1)}, s32[2048]{0:T(1024)S(1)}, /*index...) while((s32[]{:T(128)}, f32[512,3,64]{0,2,1:T(8,128)}, ...), condition=%wide.region_10.10_spmd.clone, body=%wide.region_9.9_spmd.clone.sunk | while | flops 205717504 | bytes 1926848 | solution.py:96
  174.3 12.5 %while.128 = (s32[]{:T(128)}, f32[512,3,64]{0,2,1:T(8,128)}, bf16[2048,3,64]{0,2,1:T(8,128)(2,1)S(1)}, s32[512]{0:T(512)S(1)}, s32[2048]{0:T(1024)S(1)}, /*index...) while((s32[]{:T(128)}, f32[512,3,64]{0,2,1:T(8,128)}, ...), condition=%wide.region_10.10_spmd.clone, body=%wide.region_9.9_spmd.clone.sunk | while | flops 205717504 | bytes 1926848 | solution.py:96
  195.6 118.2 %all-reduce.8.cloned.1.call-done = f32[2048,768]{0,1:T(8,128)} async-done(((f32[2048,768]{0,1:T(8,128)}), f32[2048,768]{0,1:T(8,128)}) %all-reduce.8.cloned.1.call-update) | async-done | bytes 6291472 | tf_op jit(solution)/shard_map/psum | solution.py:237
  323.0 18.8 %multiply_convert_fusion = (bf16[2048,768]{1,0:T(8,128)(2,1)}, f32[2048,768]{1,0:T(8,128)}, f32[2048,768]{1,0:T(8,128)}) fusion(f32[768]{0:T(1024)S(1)} %copy-done.63, bf16[2048,768]{0,1:T(8,128)(2,1)S(1)} %add_convert_fusion.2, bf16[768,768]{1,0:T(8,128)(2,1)S(1)} %copy-done), kind=kOutput, calls=%fused_computation.93 | convolution fusion | flops 2519728128 | bytes 20057088 | tf_op jit(solution)/shard_map/dot_general | solution.py:240
  341.8 8.1 convert_reduce_fusion.1
  370.1 105.9 %all-reduce.10.cloned.1.call-done = f32[2048,768]{0,1:T(8,128)} async-done(((f32[2048,768]{0,1:T(8,128)}), f32[2048,768]{0,1:T(8,128)}) %all-reduce.10.cloned.1.call-update) | async-done | bytes 6291472 | tf_op jit(solution)/shard_map/psum | solution.py:256
  492.9 161.6 %while.126 = (s32[]{:T(128)}, bf16[2048,3,64]{0,2,1:T(8,128)(2,1)}, f32[2048,3,64]{0,2,1:T(8,128)}, f32[2048,3,64]{0,2,1:T(8,128)S(1)}, bf16[2048,3,64]{0,2,1:T(...) while((s32[]{:T(128)}, bf16[2048,3,64]{0,2,1:T(8,128)(2,1)}, ...), condition=%wide.region_25.26_spmd, body=%wide.region_19.25_spmd.sunk | while | flops 716768768 | bytes 27696096 | solution.py:185
  494.7 12.6 %while.129 = (s32[]{:T(128)}, f32[3,512]{1,0:T(4,128)S(1)}, bf16[2048,3,64]{0,2,1:T(8,128)(2,1)}, bf16[512,3,64]{0,2,1:T(8,128)(2,1)S(1)}, s32[512]{0:T(512)S(1)...) while((s32[]{:T(128)}, f32[3,512]{1,0:T(4,128)S(1)}, ...), condition=%wide.region_22.22_spmd.clone, body=%wide.region_20.21_spmd.clone.sunk | while | flops 206308864 | bytes 7647441 | solution.py:134
  507.3 25.2 %while.130 = (s32[]{:T(128)}, f32[512,3,64]{0,2,1:T(8,128)S(1)}, f32[2048,3,64]{0,2,1:T(8,128)}, f32[2048,3,64]{0,2,1:T(8,128)S(1)}, bf16[2048,3,64]{0,2,1:T(8,1...) while((s32[]{:T(128)}, f32[512,3,64]{0,2,1:T(8,128)S(1)}, ...), condition=%wide.region_24.24_spmd.clone, body=%wide.region_23.23_spmd.clone.sunk | while | flops 510459904 | bytes 18446580 | solution.py:180
  535.1 12.6 %while.129 = (s32[]{:T(128)}, f32[3,512]{1,0:T(4,128)S(1)}, bf16[2048,3,64]{0,2,1:T(8,128)(2,1)}, bf16[512,3,64]{0,2,1:T(8,128)(2,1)S(1)}, s32[512]{0:T(512)S(1)...) while((s32[]{:T(128)}, f32[3,512]{1,0:T(4,128)S(1)}, ...), condition=%wide.region_22.22_spmd.clone, body=%wide.region_20.21_spmd.clone.sunk | while | flops 206308864 | bytes 7647441 | solution.py:134
  547.7 25.2 %while.130 = (s32[]{:T(128)}, f32[512,3,64]{0,2,1:T(8,128)S(1)}, f32[2048,3,64]{0,2,1:T(8,128)}, f32[2048,3,64]{0,2,1:T(8,128)S(1)}, bf16[2048,3,64]{0,2,1:T(8,1...) while((s32[]{:T(128)}, f32[512,3,64]{0,2,1:T(8,128)S(1)}, ...), condition=%wide.region_24.24_spmd.clone, body=%wide.region_23.23_spmd.clone.sunk | while | flops 510459904 | bytes 18446580 | solution.py:180
  575.5 12.6 %while.129 = (s32[]{:T(128)}, f32[3,512]{1,0:T(4,128)S(1)}, bf16[2048,3,64]{0,2,1:T(8,128)(2,1)}, bf16[512,3,64]{0,2,1:T(8,128)(2,1)S(1)}, s32[512]{0:T(512)S(1)...) while((s32[]{:T(128)}, f32[3,512]{1,0:T(4,128)S(1)}, ...), condition=%wide.region_22.22_spmd.clone, body=%wide.region_20.21_spmd.clone.sunk | while | flops 206308864 | bytes 7647441 | solution.py:134
  588.1 25.2 %while.130 = (s32[]{:T(128)}, f32[512,3,64]{0,2,1:T(8,128)S(1)}, f32[2048,3,64]{0,2,1:T(8,128)}, f32[2048,3,64]{0,2,1:T(8,128)S(1)}, bf16[2048,3,64]{0,2,1:T(8,1...) while((s32[]{:T(128)}, f32[512,3,64]{0,2,1:T(8,128)S(1)}, ...), condition=%wide.region_24.24_spmd.clone, body=%wide.region_23.23_spmd.clone.sunk | while | flops 510459904 | bytes 18446580 | solution.py:180
  615.9 12.6 %while.129 = (s32[]{:T(128)}, f32[3,512]{1,0:T(4,128)S(1)}, bf16[2048,3,64]{0,2,1:T(8,128)(2,1)}, bf16[512,3,64]{0,2,1:T(8,128)(2,1)S(1)}, s32[512]{0:T(512)S(1)...) while((s32[]{:T(128)}, f32[3,512]{1,0:T(4,128)S(1)}, ...), condition=%wide.region_22.22_spmd.clone, body=%wide.region_20.21_spmd.clone.sunk | while | flops 206308864 | bytes 7647441 | solution.py:134
  628.4 25.2 %while.130 = (s32[]{:T(128)}, f32[512,3,64]{0,2,1:T(8,128)S(1)}, f32[2048,3,64]{0,2,1:T(8,128)}, f32[2048,3,64]{0,2,1:T(8,128)S(1)}, bf16[2048,3,64]{0,2,1:T(8,1...) while((s32[]{:T(128)}, f32[512,3,64]{0,2,1:T(8,128)S(1)}, ...), condition=%wide.region_24.24_spmd.clone, body=%wide.region_23.23_spmd.clone.sunk | while | flops 510459904 | bytes 18446580 | solution.py:180
  682.7 100.5 %all-reduce.14.cloned.1.call-done = (bf16[2048,768]{0,1:T(8,128)(2,1)}, bf16[2048,768]{0,1:T(8,128)(2,1)}) async-done(((bf16[2048,768]{0,1:T(8,128)(2,1)}, bf16[2048,768]{0,1:T(8,128)(2,1)}), (bf16[2048,768]{0,1:T(8,128)(2,1)}, bf16[2048,768]{0,1:T(8,128)(2,1)})) %all-reduce.14.cloned.1.call-update) | async-done | bytes 6291472 | tf_op jit(solution)/shard_map/psum | solution.py:244
  811.0 13.1 %scatter_custom_fusion = f32[8193,128]{1,0:T(8,128)} fusion(s32[2048]{0:T(1024)} %get-tuple-element.1347, f32[]{:T(128)} %constant.325.clone.1, f32[2048,128]{1,0:T(8,128)} %get-tuple-element.1355, f32[]{:T(128)S(6)} %div.136), kind=kCustom, calls=%fused_computation.122 | custom fusion | flops 524288 | bytes 5243908 | tf_op jit(solution)/shard_map/scatter-add | solution.py:290
  847.8 40.1 %all-reduce = (f32[768]{0:T(1024)}, f32[768]{0:T(1024)}, f32[768]{0:T(1024)}, f32[768]{0:T(1024)}, f32[768]{0:T(1024)}, /*index=5*/f32[768]{0:T(1024)}, f32[768]{0:T(1024)}) all-reduce(f32[768]{0:T(1024)S(1)} %get-tuple-element.1324, f32[768]{0:T(1024)S(1)} %get-tuple-element.1186, ...), channel_id=1, replica_groups=mesh['dp'=8,'mp'=4] {'dp'}, use_global_device_ids=true, to_apply=%region_34.35 | all-reduce | flops 5376 | bytes 43008 | tf_op jit(solution)/shard_map/psum | solution.py:295
  887.9 172.8 %all-reduce.12.cloned.1.call-done = (f32[128,768]{1,0:T(8,128)}, f32[128,768]{1,0:T(8,128)}, f32[3,768,192]{1,2,0:T(8,128)}, f32[192,768]{1,0:T(8,128)}, f32[768,768]{1,0:T(8,128)}, /*index=5*/f32[768,768]{1,0:T(8,128)}) async-done(((f32[128,768]{1,0:T(8,128)}, f32[128,768]{1,0:T(8,128)}, f32[3,768,192]{1,2,0:T(8,128)}, f32[192,768]{1,0:T(8,128)}, f32[768,768]{1,0:T(8,128)}, ...) | async-done | bytes 7864336 | tf_op jit(solution)/shard_map/psum | solution.py:295
  1060.6 91.4 %reduce-scatter.2.cloned.1.call-done = f32[1024,128]{1,0:T(8,128)} async-done(((f32[8192,128]{1,0:T(8,128)}), f32[1024,128]{1,0:T(8,128)}) %reduce-scatter.2.cloned.1.call-update) | async-done | bytes 524304 | tf_op jit(solution)/shard_map/reduce_scatter | solution.py:291
  (643 shorter events, 459.9 us)
Async XLA Ops:
  7.2 315.8 %copy-start = (bf16[768,768]{1,0:T(8,128)(2,1)S(1)}, bf16[768,768]{1,0:T(8,128)(2,1)}, u32[]{:S(2)}) copy-start(bf16[768,768]{1,0:T(8,128)(2,1)} %param.45) | copy-start | bytes 3538948
  7.2 54.8 %all-gather.2.cloned.1.call-start = ((), (), s32[]{:S(2)}) async-start(), calls=%async_computation.1 | async-start | bytes 2359296 | tf_op jit(solution)/shard_map/all_gather | solution.py:209
  7.9 305.9 %all-reduce.8.cloned.1.call-start = ((), (), s32[]{:S(2)}) async-start(), calls=%async_computation.2 | async-start | bytes 12582912 | tf_op jit(solution)/shard_map/psum | solution.py:237
  9.4 68.8 %copy-start.51 = (pred[2048]{0:T(1024)(128)(4,1)}, pred[2048]{0:T(1024)(128)(4,1)S(1)}, u32[]{:S(2)}) copy-start(pred[2048]{0:T(1024)(128)(4,1)S(1)} %compare_and_fusion) | copy-start | bytes 6148
  11.4 66.8 %copy-start.39 = (f32[2048]{0:T(1024)}, f32[2048]{0:T(1024)S(1)}, u32[]{:S(2)}) copy-start(f32[2048]{0:T(1024)S(1)} %get-tuple-element.1349) | copy-start | bytes 24580
  13.5 69.2 %copy-start.23 = (bf16[2048,64]{0,1:T(8,128)(2,1)}, bf16[2048,64]{0,1:T(8,128)(2,1)S(1)}, u32[]{:S(2)}) copy-start(bf16[2048,64]{0,1:T(8,128)(2,1)S(1)} %get-tuple-element.1345) | copy-start | bytes 786436
  13.5 69.2 %copy-start.25 = (bf16[2048,64]{0,1:T(8,128)(2,1)}, bf16[2048,64]{0,1:T(8,128)(2,1)S(1)}, u32[]{:S(2)}) copy-start(bf16[2048,64]{0,1:T(8,128)(2,1)S(1)} %get-tuple-element.1346) | copy-start | bytes 786436
  90.5 101.3 %copy-start.29 = (bf16[192,768]{1,0:T(8,128)(2,1)S(1)}, bf16[192,768]{1,0:T(8,128)(2,1)}, u32[]{:S(2)}) copy-start(bf16[192,768]{1,0:T(8,128)(2,1)} %param.42) | copy-start | bytes 884740
  195.6 280.5 %all-reduce.10.cloned.1.call-start = ((), (), s32[]{:S(2)}) async-start(), calls=%async_computation.3 | async-start | bytes 12582912 | tf_op jit(solution)/shard_map/psum | solution.py:256
  320.8 20.9 %slice-start.2 = ((s8[6291456]{0:T(1024)(128)(4,1)}), s8[4194304]{0:T(1024)(128)(4,1)S(1)}, s32[]{:S(2)}) async-start(s8[6291456]{0:T(1024)(128)(4,1)} %bitcast.204), calls=%async_computation.9 | async-start | bytes 8388608
  322.9 18.8 %copy-start.21 = (bf16[2048,768]{0,1:T(8,128)(2,1)}, bf16[2048,768]{0,1:T(8,128)(2,1)S(1)}, u32[]{:S(2)}) copy-start(bf16[2048,768]{0,1:T(8,128)(2,1)S(1)} %add_convert_fusion.2) | copy-start | bytes 9437188
  322.9 18.8 %slice-start.3 = ((s8[6291456]{0:T(1024)(128)(4,1)}), s8[2097152]{0:T(1024)(128)(4,1)S(1)}, s32[]{:S(2)}) async-start(s8[6291456]{0:T(1024)(128)(4,1)} %bitcast.204), calls=%async_computation.10 | async-start | bytes 4194304
  322.9 18.8 %copy-start.61 = (bf16[768,768]{1,0:T(8,128)(2,1)S(1)}, bf16[768,768]{1,0:T(8,128)(2,1)}, u32[]{:S(2)}) copy-start(bf16[768,768]{1,0:T(8,128)(2,1)} %param.47) | copy-start | bytes 3538948
  356.1 427.0 %all-reduce.14.cloned.1.call-start = ((), (), s32[]{:S(2)}) async-start(), calls=%async_computation.6 | async-start | bytes 12582912 | tf_op jit(solution)/shard_map/psum | solution.py:244
  663.2 397.5 %all-reduce.12.cloned.1.call-start = ((), (), s32[]{:S(2)}) async-start(), calls=%async_computation.5 | async-start | bytes 15728640 | tf_op jit(solution)/shard_map/psum | solution.py:295
  679.4 103.8 %copy-start.38 = (f32[2048]{0:T(1024)S(1)}, f32[2048]{0:T(1024)}, u32[]{:S(2)}) copy-start(f32[2048]{0:T(1024)} %copy-done.37) | copy-start | bytes 24580
  679.4 103.7 %copy-start.50 = (f32[768]{0:T(1024)S(1)}, f32[768]{0:T(1024)}, u32[]{:S(2)}) copy-start(f32[768]{0:T(1024)} %param.39) | copy-start | bytes 9220
  679.4 115.2 %slice-start.6 = ((s8[6291456]{0:T(1024)(128)(4,1)}), s8[2097152]{0:T(1024)(128)(4,1)S(1)}, s32[]{:S(2)}) async-start(s8[6291456]{0:T(1024)(128)(4,1)} %bitcast.208), calls=%async_computation.13 | async-start | bytes 4194304
  682.7 106.2 %copy-start.48 = (f32[2048]{0:T(1024)S(1)}, f32[2048]{0:T(1024)}, u32[]{:S(2)}) copy-start(f32[2048]{0:T(1024)} %copy-done.47) | copy-start | bytes 24580
  682.7 106.3 %copy-start.44 = (f32[2048]{0:T(1024)S(1)}, f32[2048]{0:T(1024)}, u32[]{:S(2)}) copy-start(f32[2048]{0:T(1024)} %copy-done.43) | copy-start | bytes 24580
  804.5 19.6 %copy-start.11 = (bf16[8192,128]{1,0:T(8,128)(2,1)S(1)}, bf16[8192,128]{1,0:T(8,128)(2,1)}, u32[]{:S(2)}) copy-start(bf16[8192,128]{1,0:T(8,128)(2,1)} %all-gather.2.cloned.1.call-done) | copy-start | bytes 6291460
  804.5 19.6 %copy-start.42 = (f32[8192]{0:T(1024)S(1)}, f32[8192]{0:T(1024)}, u32[]{:S(2)}) copy-start(f32[8192]{0:T(1024)} %get-tuple-element.1343) | copy-start | bytes 98308
  804.5 347.5 %reduce-scatter.2.cloned.1.call-start = ((), (), s32[]{:S(2)}) async-start(), calls=%async_computation.4 | async-start | bytes 4718592 | tf_op jit(solution)/shard_map/reduce_scatter | solution.py:291
  1060.6 101.3 %copy-start.27 = (f32[768,768]{1,0:T(8,128)S(1)}, f32[768,768]{1,0:T(8,128)}, u32[]{:S(2)}) copy-start(f32[768,768]{1,0:T(8,128)} %get-tuple-element.2138) | copy-start | bytes 7077892
  (55 other events, 260.4 us)
Sparse Core Ops, SparseCore 0:
  10.1 51.7 all-gather.1
  195.7 118.1 all-reduce.7
  356.2 119.7 all-reduce.9
  663.3 119.7 all-reduce.13
  804.6 256.0 all-reduce.11
  1064.7 87.2 reduce-scatter.1
where the time goes:
time: 1180 us; the launch traced here: 1170 us
  waiting for transfers between devices  638 us (54%)
  matrix products  279 us (24%)
  other arithmetic  115 us (10%)
  local copies, waits for them, and re-layouts  75.5 us (6%)
  blocking collectives  40.1 us (3%)
  between operations  17.5 us (1%)
    psum x1, waiting for transfers between devices, body(): lax.psum((grad_w_in, grad_b_in, grad_w_time, grad_gain1, grad_shift1, gra...  173 us
    psum x1, waiting for transfers between devices, body(): resid = hidden + lax.psum(attn_part, 'mp')  118 us
    psum x1, waiting for transfers between devices, body(): grad_act_two = lax.psum(grad_two_part, 'mp')  106 us
    psum x1, waiting for transfers between devices, body(): lax.psum(down_part.astype(jnp.bfloat16), 'mp').astype(jnp.float32)  100 us
    reduce_scatter x1, waiting for transfers between devices, body(): lax.psum_scatter(direct + norm_coeff * unit_rows, 'dp', scatter_dimension...  91.4 us
    dot_general x32, matrix products, probs_for(): jnp.einsum('qhd,khd->hqk', grad_blk, value_blk, preferred_element_type=jn...  59.4 us
    all_gather x1, waiting for transfers between devices, body(): whole_table = lax.all_gather(table, 'dp', axis=0, tiled=True)  48.5 us
    dot_general x16, matrix products, value_step(): jnp.einsum('hqk,khd->qhd', weights_bf, block_rows(values_all, k_index, bl...  45.2 us
  transfers between devices with their start and end apart: 6, of which 6 were waited for; matrix products, arithmetic and copies ran while one was open for 7% of the time, Pallas kernels for 0%

commit v1 on v0

--- a/solution.py
+++ b/solution.py
@@ -8,6 +8,16 @@
 TSTEPS = 2000
 QBLK = 512
 NEG_BIG = -1000000000.0
+
+
+def collect(x, axis, dim):
+    ways, here, step = (lax.axis_size(axis), lax.axis_index(axis), x.shape[dim])
+    lengths = [n * ways if d == dim else n for d, n in enumerate(x.shape)]
+    full = lax.dynamic_update_slice_in_dim(jnp.zeros(lengths, x.dtype), x, here * step, axis=dim)
+    for far in range(1, ways):
+        x = lax.ppermute(x, axis, [(d, (d + 1) % ways) for d in range(ways)])
+        full = lax.dynamic_update_slice_in_dim(full, x, (here - far) % ways * step, axis=dim)
+    return full
 
 
 def layer_norm(inputs, gain_vec, shift_vec):
@@ -206,7 +216,7 @@
     b_down,
     cotangent,
 ):
-    whole_table = lax.all_gather(table, "dp", axis=0, tiled=True)
+    whole_table = collect(table, "dp", 0)
     table_full = whole_table.astype(jnp.float32)
     vocab_rows, embed_width = table_full.shape
     row_norms = jnp.sqrt(jnp.sum(table_full * table_full, axis=1) + 1e-06)

time: 1180 us -> 1190 us (level)
    ppermute x0 -> x7, waiting for transfers between devices: none -> 52.7 us  [collect(): x = lax.ppermute(x, axis, [(d, (d + 1) % ways) for d in range(ways)])]
    all_gather x1 -> x0, waiting for transfers between devices: 48.5 us -> none  [body(): whole_table = lax.all_gather(table, 'dp', axis=0, tiled=True)]
    unnamed x155 -> x165, local copies, waits for them, and re-layouts: 32.4 us -> 32.7 us
  transfers between devices with their start and end apart: 6 -> 12, of which waited for: 6 -> 12; matrix products, arithmetic and copies ran while one was open for 7% -> 7% of each run, Pallas kernels for 0% -> 0%
where the time goes in v1:
time: 1190 us; the launch traced here: 1180 us
  waiting for transfers between devices  638 us (54%)
  matrix products  279 us (23%)
  other arithmetic  113 us (9%)
  local copies, waits for them, and re-layouts  85.2 us (7%)
  blocking collectives  40.3 us (3%)
  between operations  17.2 us (1%)
    psum x1, waiting for transfers between devices, body(): lax.psum((grad_w_in, grad_b_in, grad_w_time, grad_gain1, grad_shift1, gra...  171 us
    psum x1, waiting for transfers between devices, body(): resid = hidden + lax.psum(attn_part, 'mp')  117 us
    psum x1, waiting for transfers between devices, body(): grad_act_two = lax.psum(grad_two_part, 'mp')  106 us
    psum x1, waiting for transfers between devices, body(): lax.psum(down_part.astype(jnp.bfloat16), 'mp').astype(jnp.float32)  100 us
    reduce_scatter x1, waiting for transfers between devices, body(): lax.psum_scatter(direct + norm_coeff * unit_rows, 'dp', scatter_dimension...  91.4 us
    dot_general x32, matrix products, probs_for(): jnp.einsum('qhd,khd->hqk', grad_blk, value_blk, preferred_element_type=jn...  59.4 us
    ppermute x7, waiting for transfers between devices, collect(): x = lax.ppermute(x, axis, [(d, (d + 1) % ways) for d in range(ways)])  52.7 us
    dot_general x16, matrix products, value_step(): jnp.einsum('hqk,khd->qhd', weights_bf, block_rows(values_all, k_index, bl...  45.2 us
  transfers between devices with their start and end apart: 12, of which 12 were waited for; matrix products, arithmetic and copies ran while one was open for 7% of the time, Pallas kernels for 0%

profile of v1, /device:TPU:0, one launch (start us, length us, event | category | flops | bytes accessed | tf_op | source)
XLA Modules:
  0.0 1182.1 jit_solution(16861523187024260218)
XLA Ops:
  10.3 9.6 collective-permute-done
  82.3 10.7 gather_fusion
  106.7 98.0 %while.123 = (s32[]{:T(128)}, bf16[4,512,3,64]{1,3,2,0:T(8,128)(2,1)}, f32[4,3,512]{2,1,0:T(4,128)}, f32[4,3,512]{2,1,0:T(4,128)}, s32[4]{0:T(128)S(1)}, /*index...) while((s32[]{:T(128)}, ...), condition=%wide.region_11.12_spmd, body=%wide.region_4.11_spmd.sunk | while | flops 312155648 | bytes 10699101 | solution.py:111
  117.0 12.5 %while.128 = (s32[]{:T(128)}, f32[512,3,64]{0,2,1:T(8,128)}, bf16[2048,3,64]{0,2,1:T(8,128)(2,1)S(1)}, s32[512]{0:T(512)S(1)}, s32[2048]{0:T(1024)S(1)}, /*index...) while((s32[]{:T(128)}, f32[512,3,64]{0,2,1:T(8,128)}, ...), condition=%wide.region_10.10_spmd.clone, body=%wide.region_9.9_spmd.clone.sunk | while | flops 205717504 | bytes 1926848 | solution.py:106
  141.5 12.5 %while.128 = (s32[]{:T(128)}, f32[512,3,64]{0,2,1:T(8,128)}, bf16[2048,3,64]{0,2,1:T(8,128)(2,1)S(1)}, s32[512]{0:T(512)S(1)}, s32[2048]{0:T(1024)S(1)}, /*index...) while((s32[]{:T(128)}, f32[512,3,64]{0,2,1:T(8,128)}, ...), condition=%wide.region_10.10_spmd.clone, body=%wide.region_9.9_spmd.clone.sunk | while | flops 205717504 | bytes 1926848 | solution.py:106
  166.0 12.5 %while.128 = (s32[]{:T(128)}, f32[512,3,64]{0,2,1:T(8,128)}, bf16[2048,3,64]{0,2,1:T(8,128)(2,1)S(1)}, s32[512]{0:T(512)S(1)}, s32[2048]{0:T(1024)S(1)}, /*index...) while((s32[]{:T(128)}, f32[512,3,64]{0,2,1:T(8,128)}, ...), condition=%wide.region_10.10_spmd.clone, body=%wide.region_9.9_spmd.clone.sunk | while | flops 205717504 | bytes 1926848 | solution.py:106
  190.5 12.5 %while.128 = (s32[]{:T(128)}, f32[512,3,64]{0,2,1:T(8,128)}, bf16[2048,3,64]{0,2,1:T(8,128)(2,1)S(1)}, s32[512]{0:T(512)S(1)}, s32[2048]{0:T(1024)S(1)}, /*index...) while((s32[]{:T(128)}, f32[512,3,64]{0,2,1:T(8,128)}, ...), condition=%wide.region_10.10_spmd.clone, body=%wide.region_9.9_spmd.clone.sunk | while | flops 205717504 | bytes 1926848 | solution.py:106
  211.8 116.6 %all-reduce.8.cloned.1.call-done = f32[2048,768]{0,1:T(8,128)} async-done(((f32[2048,768]{0,1:T(8,128)}), f32[2048,768]{0,1:T(8,128)}) %all-reduce.8.cloned.1.call-update) | async-done | bytes 6291472 | tf_op jit(solution)/shard_map/psum | solution.py:247
  337.5 18.8 %multiply_convert_fusion = (bf16[2048,768]{1,0:T(8,128)(2,1)}, f32[2048,768]{1,0:T(8,128)}, f32[2048,768]{1,0:T(8,128)}) fusion(f32[768]{0:T(1024)S(1)} %copy-done.68, bf16[2048,768]{0,1:T(8,128)(2,1)S(1)} %add_convert_fusion.2, bf16[768,768]{1,0:T(8,128)(2,1)S(1)} %copy-done), kind=kOutput, calls=%fused_computation.93 | convolution fusion | flops 2519728128 | bytes 20057088 | tf_op jit(solution)/shard_map/dot_general | solution.py:250
  384.9 105.9 %all-reduce.10.cloned.1.call-done = f32[2048,768]{0,1:T(8,128)} async-done(((f32[2048,768]{0,1:T(8,128)}), f32[2048,768]{0,1:T(8,128)}) %all-reduce.10.cloned.1.call-update) | async-done | bytes 6291472 | tf_op jit(solution)/shard_map/psum | solution.py:266
  507.6 161.5 %while.126 = (s32[]{:T(128)}, bf16[2048,3,64]{0,2,1:T(8,128)(2,1)}, f32[2048,3,64]{0,2,1:T(8,128)}, f32[2048,3,64]{0,2,1:T(8,128)S(1)}, bf16[2048,3,64]{0,2,1:T(...) while((s32[]{:T(128)}, bf16[2048,3,64]{0,2,1:T(8,128)(2,1)}, ...), condition=%wide.region_25.26_spmd, body=%wide.region_19.25_spmd.sunk | while | flops 716768768 | bytes 27696096 | solution.py:195
  509.4 12.6 %while.129 = (s32[]{:T(128)}, f32[3,512]{1,0:T(4,128)S(1)}, bf16[2048,3,64]{0,2,1:T(8,128)(2,1)}, bf16[512,3,64]{0,2,1:T(8,128)(2,1)S(1)}, s32[512]{0:T(512)S(1)...) while((s32[]{:T(128)}, f32[3,512]{1,0:T(4,128)S(1)}, ...), condition=%wide.region_22.22_spmd.clone, body=%wide.region_20.21_spmd.clone.sunk | while | flops 206308864 | bytes 7647441 | solution.py:144
  522.0 25.2 %while.130 = (s32[]{:T(128)}, f32[512,3,64]{0,2,1:T(8,128)S(1)}, f32[2048,3,64]{0,2,1:T(8,128)}, f32[2048,3,64]{0,2,1:T(8,128)S(1)}, bf16[2048,3,64]{0,2,1:T(8,1...) while((s32[]{:T(128)}, f32[512,3,64]{0,2,1:T(8,128)S(1)}, ...), condition=%wide.region_24.24_spmd.clone, body=%wide.region_23.23_spmd.clone.sunk | while | flops 510459904 | bytes 18446580 | solution.py:190
  549.8 12.6 %while.129 = (s32[]{:T(128)}, f32[3,512]{1,0:T(4,128)S(1)}, bf16[2048,3,64]{0,2,1:T(8,128)(2,1)}, bf16[512,3,64]{0,2,1:T(8,128)(2,1)S(1)}, s32[512]{0:T(512)S(1)...) while((s32[]{:T(128)}, f32[3,512]{1,0:T(4,128)S(1)}, ...), condition=%wide.region_22.22_spmd.clone, body=%wide.region_20.21_spmd.clone.sunk | while | flops 206308864 | bytes 7647441 | solution.py:144
  562.3 25.2 %while.130 = (s32[]{:T(128)}, f32[512,3,64]{0,2,1:T(8,128)S(1)}, f32[2048,3,64]{0,2,1:T(8,128)}, f32[2048,3,64]{0,2,1:T(8,128)S(1)}, bf16[2048,3,64]{0,2,1:T(8,1...) while((s32[]{:T(128)}, f32[512,3,64]{0,2,1:T(8,128)S(1)}, ...), condition=%wide.region_24.24_spmd.clone, body=%wide.region_23.23_spmd.clone.sunk | while | flops 510459904 | bytes 18446580 | solution.py:190
  590.1 12.6 %while.129 = (s32[]{:T(128)}, f32[3,512]{1,0:T(4,128)S(1)}, bf16[2048,3,64]{0,2,1:T(8,128)(2,1)}, bf16[512,3,64]{0,2,1:T(8,128)(2,1)S(1)}, s32[512]{0:T(512)S(1)...) while((s32[]{:T(128)}, f32[3,512]{1,0:T(4,128)S(1)}, ...), condition=%wide.region_22.22_spmd.clone, body=%wide.region_20.21_spmd.clone.sunk | while | flops 206308864 | bytes 7647441 | solution.py:144
  602.7 25.2 %while.130 = (s32[]{:T(128)}, f32[512,3,64]{0,2,1:T(8,128)S(1)}, f32[2048,3,64]{0,2,1:T(8,128)}, f32[2048,3,64]{0,2,1:T(8,128)S(1)}, bf16[2048,3,64]{0,2,1:T(8,1...) while((s32[]{:T(128)}, f32[512,3,64]{0,2,1:T(8,128)S(1)}, ...), condition=%wide.region_24.24_spmd.clone, body=%wide.region_23.23_spmd.clone.sunk | while | flops 510459904 | bytes 18446580 | solution.py:190
  630.5 12.5 %while.129 = (s32[]{:T(128)}, f32[3,512]{1,0:T(4,128)S(1)}, bf16[2048,3,64]{0,2,1:T(8,128)(2,1)}, bf16[512,3,64]{0,2,1:T(8,128)(2,1)S(1)}, s32[512]{0:T(512)S(1)...) while((s32[]{:T(128)}, f32[3,512]{1,0:T(4,128)S(1)}, ...), condition=%wide.region_22.22_spmd.clone, body=%wide.region_20.21_spmd.clone.sunk | while | flops 206308864 | bytes 7647441 | solution.py:144
  643.0 25.2 %while.130 = (s32[]{:T(128)}, f32[512,3,64]{0,2,1:T(8,128)S(1)}, f32[2048,3,64]{0,2,1:T(8,128)}, f32[2048,3,64]{0,2,1:T(8,128)S(1)}, bf16[2048,3,64]{0,2,1:T(8,1...) while((s32[]{:T(128)}, f32[512,3,64]{0,2,1:T(8,128)S(1)}, ...), condition=%wide.region_24.24_spmd.clone, body=%wide.region_23.23_spmd.clone.sunk | while | flops 510459904 | bytes 18446580 | solution.py:190
  695.7 100.5 %all-reduce.14.cloned.1.call-done = (bf16[2048,768]{0,1:T(8,128)(2,1)}, bf16[2048,768]{0,1:T(8,128)(2,1)}) async-done(((bf16[2048,768]{0,1:T(8,128)(2,1)}, bf16[2048,768]{0,1:T(8,128)(2,1)}), (bf16[2048,768]{0,1:T(8,128)(2,1)}, bf16[2048,768]{0,1:T(8,128)(2,1)})) %all-reduce.14.cloned.1.call-update) | async-done | bytes 6291472 | tf_op jit(solution)/shard_map/psum | solution.py:254
  825.2 13.1 %scatter_custom_fusion = f32[8193,128]{1,0:T(8,128)} fusion(s32[2048]{0:T(1024)} %get-tuple-element.1347, f32[]{:T(128)} %constant.392.clone.1, f32[2048,128]{1,0:T(8,128)} %get-tuple-element.1355, f32[]{:T(128)S(6)} %div.136), kind=kCustom, calls=%fused_computation.122 | custom fusion | flops 524288 | bytes 5243908 | tf_op jit(solution)/shard_map/scatter-add | solution.py:300
  862.2 40.3 %all-reduce = (f32[768]{0:T(1024)}, f32[768]{0:T(1024)}, f32[768]{0:T(1024)}, f32[768]{0:T(1024)}, f32[768]{0:T(1024)}, /*index=5*/f32[768]{0:T(1024)}, f32[768]{0:T(1024)}) all-reduce(f32[768]{0:T(1024)S(1)} %get-tuple-element.1324, f32[768]{0:T(1024)S(1)} %get-tuple-element.1186, ...), channel_id=1, replica_groups=mesh['dp'=8,'mp'=4] {'dp'}, use_global_device_ids=true, to_apply=%region_34.35 | all-reduce | flops 5376 | bytes 43008 | tf_op jit(solution)/shard_map/psum | solution.py:305
  902.5 171.4 %all-reduce.12.cloned.1.call-done = (f32[128,768]{1,0:T(8,128)}, f32[128,768]{1,0:T(8,128)}, f32[3,768,192]{1,2,0:T(8,128)}, f32[192,768]{1,0:T(8,128)}, f32[768,768]{1,0:T(8,128)}, /*index=5*/f32[768,768]{1,0:T(8,128)}) async-done(((f32[128,768]{1,0:T(8,128)}, f32[128,768]{1,0:T(8,128)}, f32[3,768,192]{1,2,0:T(8,128)}, f32[192,768]{1,0:T(8,128)}, f32[768,768]{1,0:T(8,128)}, ...) | async-done | bytes 7864336 | tf_op jit(solution)/shard_map/psum | solution.py:305
  1073.8 91.4 %reduce-scatter.2.cloned.1.call-done = f32[1024,128]{1,0:T(8,128)} async-done(((f32[8192,128]{1,0:T(8,128)}), f32[1024,128]{1,0:T(8,128)}) %reduce-scatter.2.cloned.1.call-update) | async-done | bytes 524304 | tf_op jit(solution)/shard_map/reduce_scatter | solution.py:301
  (673 shorter events, 511.3 us)
Async XLA Ops:
  7.2 330.3 %copy-start = (bf16[768,768]{1,0:T(8,128)(2,1)S(1)}, bf16[768,768]{1,0:T(8,128)(2,1)}, u32[]{:S(2)}) copy-start(bf16[768,768]{1,0:T(8,128)(2,1)} %param.45) | copy-start | bytes 3538948
  7.2 321.2 %all-reduce.8.cloned.1.call-start = ((), (), s32[]{:S(2)}) async-start(), calls=%async_computation.1 | async-start | bytes 12582912 | tf_op jit(solution)/shard_map/psum | solution.py:247
  7.2 12.6 %collective-permute-start = (bf16[1024,128]{1,0:T(8,128)(2,1)}, bf16[1024,128]{1,0:T(8,128)(2,1)S(1)}, u32[]{:S(2)}, u32[]{:S(2)}) collective-permute-start(bf16[1024,128]{1,0:T(8,128)(2,1)} %param.35), channel_id=1, source_target_pairs={{0,4},{4,8},{8,12},{12,16},{16,20},{20,24},{24,28},{28,0},{1,5},{5... | collective-permute-start | bytes 786440 | tf_op jit(solution)/shard_map/ppermute | solution.py:18
  19.8 10.2 collective-permute-start.1
  30.0 9.3 collective-permute-start.2
  33.4 65.5 %copy-start.23 = (bf16[2048,64]{0,1:T(8,128)(2,1)}, bf16[2048,64]{0,1:T(8,128)(2,1)S(1)}, u32[]{:S(2)}) copy-start(bf16[2048,64]{0,1:T(8,128)(2,1)S(1)} %get-tuple-element.1345) | copy-start | bytes 786436
  39.3 9.2 collective-permute-start.3
  40.0 52.9 %copy-start.55 = (pred[2048]{0:T(1024)(128)(4,1)}, pred[2048]{0:T(1024)(128)(4,1)S(1)}, u32[]{:S(2)}) copy-start(pred[2048]{0:T(1024)(128)(4,1)S(1)} %compare_and_fusion) | copy-start | bytes 6148
  48.5 9.4 collective-permute-start.4
  51.3 41.7 %copy-start.43 = (f32[2048]{0:T(1024)}, f32[2048]{0:T(1024)S(1)}, u32[]{:S(2)}) copy-start(f32[2048]{0:T(1024)S(1)} %get-tuple-element.1349) | copy-start | bytes 24580
  57.9 9.9 collective-permute-start.5
  67.8 9.1 collective-permute-start.6
  106.7 101.1 %copy-start.29 = (bf16[192,768]{1,0:T(8,128)(2,1)S(1)}, bf16[192,768]{1,0:T(8,128)(2,1)}, u32[]{:S(2)}) copy-start(bf16[192,768]{1,0:T(8,128)(2,1)} %param.42) | copy-start | bytes 884740
  211.6 279.1 %all-reduce.10.cloned.1.call-start = ((), (), s32[]{:S(2)}) async-start(), calls=%async_computation.2 | async-start | bytes 12582912 | tf_op jit(solution)/shard_map/psum | solution.py:266
  335.4 20.9 %slice-start.2 = ((s8[6291456]{0:T(1024)(128)(4,1)}), s8[4194304]{0:T(1024)(128)(4,1)S(1)}, s32[]{:S(2)}) async-start(s8[6291456]{0:T(1024)(128)(4,1)} %bitcast.204), calls=%async_computation.8 | async-start | bytes 8388608
  337.5 18.9 %copy-start.21 = (bf16[2048,768]{0,1:T(8,128)(2,1)}, bf16[2048,768]{0,1:T(8,128)(2,1)S(1)}, u32[]{:S(2)}) copy-start(bf16[2048,768]{0,1:T(8,128)(2,1)S(1)} %add_convert_fusion.2) | copy-start | bytes 9437188
  337.5 18.9 %slice-start.3 = ((s8[6291456]{0:T(1024)(128)(4,1)}), s8[2097152]{0:T(1024)(128)(4,1)S(1)}, s32[]{:S(2)}) async-start(s8[6291456]{0:T(1024)(128)(4,1)} %bitcast.204), calls=%async_computation.9 | async-start | bytes 4194304
  370.8 425.4 %all-reduce.14.cloned.1.call-start = ((), (), s32[]{:S(2)}) async-start(), calls=%async_computation.5 | async-start | bytes 12582912 | tf_op jit(solution)/shard_map/psum | solution.py:254
  676.2 397.6 %all-reduce.12.cloned.1.call-start = ((), (), s32[]{:S(2)}) async-start(), calls=%async_computation.4 | async-start | bytes 15728640 | tf_op jit(solution)/shard_map/psum | solution.py:305
  692.4 103.8 %copy-start.39 = (f32[2048]{0:T(1024)S(1)}, f32[2048]{0:T(1024)}, u32[]{:S(2)}) copy-start(f32[2048]{0:T(1024)} %copy-done.38) | copy-start | bytes 24580
  692.4 103.7 %copy-start.54 = (f32[768]{0:T(1024)S(1)}, f32[768]{0:T(1024)}, u32[]{:S(2)}) copy-start(f32[768]{0:T(1024)} %param.39) | copy-start | bytes 9220
  692.4 115.4 %slice-start.6 = ((s8[6291456]{0:T(1024)(128)(4,1)}), s8[2097152]{0:T(1024)(128)(4,1)S(1)}, s32[]{:S(2)}) async-start(s8[6291456]{0:T(1024)(128)(4,1)} %bitcast.208), calls=%async_computation.12 | async-start | bytes 4194304
  817.6 347.6 %reduce-scatter.2.cloned.1.call-start = ((), (), s32[]{:S(2)}) async-start(), calls=%async_computation.3 | async-start | bytes 4718592 | tf_op jit(solution)/shard_map/reduce_scatter | solution.py:301
  1073.8 98.7 %copy-start.28 = (f32[768,768]{1,0:T(8,128)S(1)}, f32[768,768]{1,0:T(8,128)}, u32[]{:S(2)}) copy-start(f32[768,768]{1,0:T(8,128)} %get-tuple-element.2136) | copy-start | bytes 7077892
  (66 other events, 337.2 us)
Sparse Core Ops, SparseCore 0:
  211.7 116.6 all-reduce.7
  370.9 119.7 all-reduce.9
  676.3 119.7 all-reduce.13
  817.7 256.0 all-reduce.11
  1077.9 87.2 reduce-scatter.1
